TPU v7x, 256 devices: a whole 4x4x8 slice. The times are simulated.
256 devices in a mesh: req: 32 (over z, y), mdl: 8 (over x, core).
Axes of the slice: x: 4, y: 4, z: 8, core: 2. Of those that a mesh axis runs over, the one named last changes fastest.
Arguments:
- stream: bfloat16 [24576, 1792], P('req'), may hold values from -6 to 6
- attention_projection_weight: bfloat16 [3, 1792, 1792], P(None, 'mdl'), may hold values from -0.125 to 0.125
- head_output_weight: bfloat16 [1792, 1792], P('mdl'), may hold values from -0.125 to 0.125
- adapter_down_maps: bfloat16 [64, 1792, 16], P('mdl'), may hold values from -0.125 to 0.125
- adapter_up_maps: bfloat16 [2, 1792, 1024], P(None, 'mdl'), may hold values from -1.5 to 1.5
- tenant_adapter_scale: float32 [4], replicated, may hold values from 0.5 to 2
- feedforward_norm_gain: bfloat16 [1792], replicated, may hold values from 0.099609375 to 1.8984375
- feedforward_weight: bfloat16 [3, 1792, 4864], P(None, 'req', 'mdl'), may hold values from -0.125 to 0.125
- prefix_cache_store: bfloat16 [1024, 2, 1792, 128], P('req', None, 'mdl'), may hold values from -140 to 140
- token_adapter_index: int32 [24576], P('req'), may hold values from 0 to 63
- request_token_lengths: int32 [32, 24], P('req'), may hold values from 1 to 192, 768 in all within a row
- request_tenant_index: int32 [768], P('req'), may hold values from 0 to 3
- last_page_holder: int32 [768, 1], replicated, may hold values from 0 to 31; in each aligned block of 24 rows (0 to 23, 24 to 47, ...) at most 2 rows name the same one
- holder_page_slot: int32 [768], replicated, may hold values from 0 to 31
- page_filled_rows: int32 [768], replicated, may hold values from 64 to 128
Outputs:
- layer_out: bfloat16 [24576, 1792], P(('req', 'mdl'))
Inputs may be any that keep to these rules, and one draw needn't show every extreme that they name: `last_page_holder`: within the rows of one index of req (aligned blocks of 24 rows) no holder is named more than 2 times, and one holder exactly 2 times in some blocks. `request_token_lengths`: each row sums to 768; its longest request has exactly 192 tokens.
All inputs are finite; a program needn't handle non-finite values.
Results may differ from a plain program's by a relative error of at most 0.025.
Values may be sent and summed in bfloat16 or wider, within the bound.
A program may use at most 128 MiB of HBM per device.

v0:
```python
import math
import jax
import jax.numpy as jnp
from jax import lax
from jax.sharding import PartitionSpec as P

HEAD_SIZE = 112
WINDOW = 64


def per_device(
    stream,
    attention_projection_weight,
    head_output_weight,
    adapter_down_maps,
    adapter_up_maps,
    tenant_adapter_scale,
    feedforward_norm_gain,
    feedforward_weight,
    prefix_cache_store,
    token_adapter_index,
    request_token_lengths,
    request_tenant_index,
    last_page_holder,
    holder_page_slot,
    page_filled_rows,
):
    tok_count, model_width = stream.shape
    head_column_set = attention_projection_weight.shape[1]
    head_local = head_column_set // HEAD_SIZE
    req_per_dev = request_token_lengths.shape[1]
    rank_total_width = adapter_down_maps.shape[2]
    adapter_number = adapter_up_maps.shape[2] // rank_total_width
    req_devices = lax.axis_size("req")
    req_index = lax.axis_index("req")
    mdl_index = lax.axis_index("mdl")
    row_share = tok_count // lax.axis_size("mdl")
    cap_slots = max(2, (req_per_dev + req_devices - 1) // req_devices + 1)
    projected_rows = jnp.einsum(
        "td,kcd->ktc", stream, attention_projection_weight, preferred_element_type=jnp.float32
    )
    all_onehot = (
        token_adapter_index[:, None] == jnp.arange(adapter_number, dtype=jnp.int32)[None, :]
    )
    holder_count = adapter_down_maps.shape[0]
    holder_rank_rows = jnp.einsum(
        "qf,kfn->qkn", stream, adapter_down_maps, preferred_element_type=jnp.float32
    )
    held_onehot = (
        token_adapter_index[:, None]
        == (mdl_index * holder_count + jnp.arange(holder_count, dtype=jnp.int32))[None, :]
    )
    rank_part = jnp.sum(holder_rank_rows * held_onehot.astype(jnp.float32)[:, :, None], axis=1)
    rank_feat = lax.psum(rank_part.astype(jnp.bfloat16), "mdl")
    broadcast_result = (
        all_onehot.astype(jnp.bfloat16)[:, :, None] * rank_feat[:, None, :]
    ).reshape(tok_count, adapter_number * rank_total_width)
    adapter_column_set = jnp.einsum(
        "iu,pdu->ipd", broadcast_result, adapter_up_maps, preferred_element_type=jnp.float32
    )
    positions = jnp.arange(tok_count, dtype=jnp.int32)
    lengths_row = request_token_lengths[0]
    starts = jnp.cumsum(lengths_row) - lengths_row
    member = (positions[:, None] >= starts[None, :]) & (
        positions[:, None] < (starts + lengths_row)[None, :]
    )
    member_int = member.astype(jnp.int32)
    request_of = jnp.sum(member_int * jnp.arange(req_per_dev, dtype=jnp.int32)[None, :], axis=1)
    relative = positions - jnp.sum(member_int * starts[None, :], axis=1)
    tenant_hot = (
        request_tenant_index[:, None]
        == jnp.arange(tenant_adapter_scale.shape[0], dtype=jnp.int32)[None, :]
    ).astype(jnp.float32)
    request_scale = jnp.sum(tenant_hot * tenant_adapter_scale[None, :], axis=1)
    per_token_scale = jnp.sum(member.astype(jnp.float32) * request_scale[None, :], axis=1)[:, None]
    query_rows = (projected_rows[0] + per_token_scale * adapter_column_set[:, 0]).astype(
        jnp.bfloat16
    )
    key_rows = projected_rows[1].astype(jnp.bfloat16)
    value_row_block = (projected_rows[2] + per_token_scale * adapter_column_set[:, 1]).astype(
        jnp.bfloat16
    )
    owner_column = last_page_holder[:, 0]
    owner_table = owner_column.reshape(req_devices, req_per_dev)
    slot_table = holder_page_slot.reshape(req_devices, req_per_dev)
    owned = (owner_table == req_index).astype(jnp.int32)
    owned_rank = jnp.cumsum(owned, axis=1) - 1
    picked = owned[:, None, :] * (
        owned_rank[:, None, :] == jnp.arange(cap_slots, dtype=jnp.int32)[None, :, None]
    ).astype(jnp.int32)
    send_slot = jnp.sum(picked * slot_table[:, None, :], axis=2)
    fill_table = page_filled_rows.reshape(req_devices, req_per_dev)
    send_fill = jnp.sum(picked * fill_table[:, None, :], axis=2)
    my_owner = lax.dynamic_slice_in_dim(owner_column, req_index * req_per_dev, req_per_dev, 0)
    order_ids = jnp.arange(req_per_dev, dtype=jnp.int32)
    earlier = (my_owner[:, None] == my_owner[None, :]) & (order_ids[:, None] > order_ids[None, :])
    flat_pick = my_owner * cap_slots + jnp.sum(earlier.astype(jnp.int32), axis=1)
    page_inner = prefix_cache_store.shape[1:3]
    page_rows = prefix_cache_store.shape[3]
    pages = jnp.take(prefix_cache_store, send_slot.reshape(-1), axis=0, mode="clip")
    window_pick = (
        jnp.arange(page_rows, dtype=jnp.int32)[None, :, None]
        == send_fill.reshape(-1)[:, None, None]
        - WINDOW
        + jnp.arange(WINDOW, dtype=jnp.int32)[None, None, :]
    ).astype(jnp.bfloat16)
    source_pages = jnp.einsum(
        "skcr,srj->sjkc", pages, window_pick, preferred_element_type=jnp.float32
    ).astype(jnp.bfloat16)
    source_pages = source_pages.reshape((req_devices, cap_slots, WINDOW) + page_inner)
    arrived = lax.all_to_all(source_pages, "req", split_axis=0, concat_axis=0, tiled=True)
    prefix = jnp.take(
        arrived.reshape((req_devices * cap_slots, WINDOW) + page_inner),
        flat_pick,
        axis=0,
        mode="clip",
    )
    key_all = jnp.concatenate(
        [key_rows, prefix[:, :, 0].reshape(req_per_dev * WINDOW, head_column_set)], axis=0
    )
    value_all = jnp.concatenate(
        [value_row_block, prefix[:, :, 1].reshape(req_per_dev * WINDOW, head_column_set)], axis=0
    )
    distance = positions[:, None] - positions[None, :]
    local_ok = (request_of[:, None] == request_of[None, :]) & (distance >= 0) & (distance <= WINDOW)
    key_request = jnp.repeat(jnp.arange(req_per_dev, dtype=jnp.int32), WINDOW)
    key_offset = jnp.tile(jnp.arange(WINDOW, dtype=jnp.int32), req_per_dev)
    prefix_ok = (request_of[:, None] == key_request[None, :]) & (
        key_offset[None, :] >= relative[:, None]
    )
    allowed = jnp.concatenate([local_ok, prefix_ok], axis=1)
    query_heads = query_rows.reshape(tok_count, head_local, HEAD_SIZE)
    key_heads = key_all.reshape(-1, head_local, HEAD_SIZE)
    value_heads = value_all.reshape(-1, head_local, HEAD_SIZE)
    scores = jnp.einsum(
        "thd,shd->hts", query_heads, key_heads, preferred_element_type=jnp.float32
    ) * (1.0 / math.sqrt(HEAD_SIZE))
    masked = jnp.where(allowed[None], scores, -1e30)
    row_max = jnp.max(masked, axis=-1, keepdims=True)
    exp_scores = jnp.exp(masked - row_max)
    weights = (exp_scores / jnp.sum(exp_scores, axis=-1, keepdims=True)).astype(jnp.bfloat16)
    mixed = (
        jnp.einsum("hts,shd->thd", weights, value_heads, preferred_element_type=jnp.float32)
        .astype(jnp.bfloat16)
        .reshape(tok_count, head_column_set)
    )
    attn_part = (
        jnp.dot(mixed, head_output_weight, preferred_element_type=jnp.float32)
        .astype(jnp.bfloat16)
        .astype(jnp.float32)
    )
    gain_wide = feedforward_norm_gain.astype(jnp.float32)[None, :]
    attn_full = lax.psum(attn_part.astype(jnp.bfloat16), "mdl").astype(jnp.float32)
    resid_full = (stream.astype(jnp.float32) + attn_full).astype(jnp.bfloat16)
    resid_wide = resid_full.astype(jnp.float32)
    mean_sq = jnp.mean(resid_wide * resid_wide, axis=1, keepdims=True)
    normed = (resid_wide * lax.rsqrt(mean_sq + 1e-06) * gain_wide).astype(jnp.bfloat16)
    resid_mine = lax.dynamic_slice_in_dim(resid_full, mdl_index * row_share, row_share, 0)
    full_mlp = lax.all_gather(feedforward_weight, "req", axis=1, tiled=True)
    gate_part = jnp.dot(normed, full_mlp[0], preferred_element_type=jnp.float32)
    up_part = jnp.dot(normed, full_mlp[1], preferred_element_type=jnp.float32)
    hidden = (jax.nn.silu(gate_part) * up_part).astype(jnp.bfloat16)
    mlp_part = (
        jnp.einsum("tf,df->td", hidden, full_mlp[2], preferred_element_type=jnp.float32)
        .astype(jnp.bfloat16)
        .astype(jnp.float32)
    )
    mlp_mine = lax.psum_scatter(
        mlp_part.astype(jnp.bfloat16), "mdl", scatter_dimension=0, tiled=True
    ).astype(jnp.float32)
    return (resid_mine.astype(jnp.float32) + mlp_mine).astype(jnp.bfloat16)


def solution(mesh):
    return jax.shard_map(
        per_device,
        mesh=mesh,
        in_specs=(
            P("req", None),
            P(None, "mdl", None),
            P("mdl", None),
            P("mdl", None, None),
            P(None, "mdl", None),
            P(),
            P(),
            P(None, "req", "mdl"),
            P("req", None, "mdl", None),
            P("req"),
            P("req", None),
            P("req"),
            P(),
            P(),
            P(),
        ),
        out_specs=P(("req", "mdl"), None),
        check_vma=False,
    )
```

profile of v0, /device:TPU:8, one launch (start us, length us, event | category | flops | bytes accessed | tf_op | source)
XLA Modules:
  0.0 314.7 jit_solution(2396669354189061754)
XLA Ops:
  7.4 0.8 fusion.39
  8.2 0.1 reshape.191
  8.3 0.1 copy.24
  8.4 0.2 reduce_window_sum.18
  8.6 0.1 copy.23
  8.6 0.8 mul.159
  9.4 0.1 copy.25
  9.5 0.8 mul.162
  10.3 0.1 copy.27
  10.4 0.1 copy.28
  10.5 0.1 reshape.194
  10.6 0.1 copy.26
  10.7 0.1 sub.51
  10.8 0.1 iota_add_fusion
  10.9 6.5 %gather_fusion = bf16[64,2,224,128]{3,2,1,0:T(8,128)(2,1)} fusion(bf16[32,2,224,128]{3,2,1,0:T(8,128)(2,1)} %param.23, s32[1024]{0:T(1024)S(1)} %pad_clamp_fusion.1), kind=kCustom, calls=%fused_computation | custom fusion | bytes 14680320 | tf_op jit(solution)/shard_map/jit(_take)/gather | solution.py:100
  17.4 13.2 %convolution_convert_fusion.2 = bf16[64,64,2,224]{3,1,2,0:T(8,128)(2,1)} fusion(bf16[64,2,224,128]{3,2,1,0:T(8,128)(2,1)} %gather_fusion, s32[64,64]{1,0:T(8,128)S(1)} %iota_add_fusion), kind=kOutput, calls=%fused_computation.23 | convolution fusion | flops 472121344 | bytes 11026432 | tf_op jit(solution)/shard_map/skcr,srj->sjkc/dot_general | solution.py:107
  30.5 11.9 %all-to-all-start = ((bf16[32,2,64,2,224]{4,2,3,1,0:T(8,128)(2,1)}), bf16[32,2,64,2,224]{4,2,3,1,0:T(8,128)(2,1)}, u32[]{:S(2)}, u32[]{:S(2)}) async-start(bf16[32,2,64,2,224]{4,2,3,1,0:T(8,128)(2,1)} %bitcast.75), calls=%async_computation | async-start | bytes 8388608 | tf_op jit(solution)/shard_map/all_to_all | solution.py:111
  42.4 0.0 all-reduce.2.cloned.1.call-start
  42.5 0.1 copy.21
  42.6 0.1 reduce
  42.7 0.1 eq.156
  42.8 0.1 ge.45
  42.9 3.9 %fusion.19 = f32[3,768,224]{1,2,0:T(8,128)S(1)} fusion(bf16[3,224,1792]{2,1,0:T(8,128)(2,1)S(1)} %copy-done, bf16[768,1792]{1,0:T(8,128)(2,1)} %param.15), kind=kOutput, calls=%fused_computation.37 | convolution fusion | flops 1849688064 | bytes 7225344 | tf_op jit(solution)/shard_map/td,kcd->ktc/dot_general | solution.py:39
  46.8 1.3 copy-done.2
  48.2 0.0 copy-start.12
  48.2 0.1 compare_convert_fusion
  48.3 2.8 fusion.55
  51.2 26.8 %psum.14 = bf16[768,16]{0,1:T(8,128)(2,1)S(1)} all-reduce(bf16[768,16]{0,1:T(8,128)(2,1)S(1)} %multiply_reduce_fusion), channel_id=1, replica_groups=mesh['req'=32,'mdl'=8] {'mdl'}, use_global_device_ids=true, to_apply=%region_4.5 | all-reduce | flops 12288 | bytes 49152 | tf_op jit(solution)/shard_map/psum | solution.py:54
  78.0 0.8 fusion.42
  78.7 0.2 convert_reduce_fusion
  78.9 0.8 fusion.41
  79.7 0.1 select_reduce_fusion.3
  79.8 0.1 select_reduce_fusion.2
  79.9 0.1 select_reduce_fusion.1
  80.0 0.1 broadcast_multiply_fusion
  80.1 1.4 fusion.51
  81.6 0.9 fusion.56
  82.5 0.1 fusion.53
  82.6 0.3 fusion.14
  82.9 1.0 add_convert_fusion.3
  83.9 1.2 compare_and_fusion
  85.2 1.3 pad_add_fusion
  86.5 49.7 %all-to-all-done = bf16[32,2,64,2,224]{4,2,3,1,0:T(8,128)(2,1)} async-done(((bf16[32,2,64,2,224]{4,2,3,1,0:T(8,128)(2,1)}), bf16[32,2,64,2,224]{4,2,3,1,0:T(8,128)(2,1)}, u32[]{:S(2)}, u32[]{:S(2)}) %all-to-all-start) | async-done | bytes 3670048 | tf_op jit(solution)/shard_map/all_to_all | solution.py:111
  136.2 2.8 gather_fusion.1
  139.1 0.2 fusion.52
  139.2 0.4 concatenate.18
  139.7 0.6 copy.30
  140.3 0.4 concatenate.15
  140.7 0.6 copy.29
  141.3 9.6 %fusion.54 = (f32[2,768]{1,0:T(2,128)S(1)}, f32[2,768,2304]{2,1,0:T(8,128)}) fusion(pred[768,2304]{1,0:T(8,128)(4,1)} %pad_add_fusion, bf16[768,2,112]{0,2,1:T(8,128)(2,1)S(1)} %copy-done.6, bf16[1536,2,112]{0,2,1:T(8,128)(2,1)S(1)} %copy.30, bf16[768,2,112]{0,2,1:T(8,128)(2,1)S(1)} %bitcast.83), kind=kOutput, calls=%fused_computation.97 | convolution fusion | flops 808945920 | bytes 17307648 | tf_op jit(solution)/shard_map/sub | solution.py:140
  150.9 7.6 %fusion.24 = bf16[2,112,768]{2,1,0:T(8,128)(2,1)S(1)} fusion(f32[2,768,2304]{2,1,0:T(8,128)} %get-tuple-element.20, f32[2,768]{1,0:T(2,128)S(1)} %get-tuple-element.19, bf16[1536,2,112]{0,2,1:T(8,128)(2,1)S(1)} %copy.29, bf16[768,2,112]{0,2,1:T(8,128)(2,1)S(1)} %copy-done.5), kind=kOutput, calls=%fused_computation.39 | convolution fusion | flops 802037760 | bytes 15538176 | tf_op jit(solution)/shard_map/hts,shd->thd/dot_general | solution.py:143
  158.4 2.5 convolution_convert_fusion
  161.0 0.0 all-reduce.2.cloned.1.call-update
  161.0 0.0 all-gather.2.cloned.1.call-start
  161.1 0.5 all-gather.2.cloned.1.call-update
  161.6 0.3 reduce-scatter.2.cloned.1.call-start
  161.9 71.7 %all-reduce.2.cloned.1.call-done = bf16[768,1792]{1,0:T(8,128)(2,1)} async-done(((bf16[768,1792]{1,0:T(8,128)(2,1)}), bf16[768,1792]{1,0:T(8,128)(2,1)}) %all-reduce.2.cloned.1.call-update) | async-done | bytes 2752528 | tf_op jit(solution)/shard_map/psum | solution.py:153
  233.6 5.3 %fusion.6 = (f32[768]{0:T(1024)S(1)}, bf16[768,1792]{1,0:T(8,128)(2,1)}) fusion(bf16[768,1792]{1,0:T(8,128)(2,1)} %all-reduce.2.cloned.1.call-done, bf16[768,1792]{1,0:T(8,128)(2,1)} %param.15), kind=kLoop, calls=%fused_computation.14 | loop fusion | flops 9633024 | bytes 8260608 | tf_op jit(solution)/shard_map/reduce_sum | solution.py:156
  238.9 14.1 %all-gather.2.cloned.1.call-done = bf16[3,1792,608]{2,1,0:T(8,128)(2,1)} async-done(((bf16[3,56,608]{2,1,0:T(8,128)(2,1)}), bf16[3,1792,608]{2,1,0:T(8,128)(2,1)}) %all-gather.2.cloned.1.call-update) | async-done | bytes 6537232 | tf_op jit(solution)/shard_map/all_gather | solution.py:159
  253.0 5.8 %fusion.16 = f32[768,608]{0,1:T(8,128)} fusion(bf16[3,1792,608]{2,1,0:T(8,128)(2,1)} %all-gather.2.cloned.1.call-done, bf16[768,1792]{1,0:T(8,128)(2,1)} %get-tuple-element.10, f32[1792]{0:T(1024)S(1)} %convert_element_type.123, f32[768]{0:T(1024)S(1)} %add_rsqrt_fusion), kind=kOutput, calls=%fused_computation.33 | convolution fusion | flops 1679032320 | bytes 6924288 | tf_op jit(solution)/shard_map/dot_general | solution.py:160
  258.9 10.5 %convolution_convert_fusion.1 = bf16[768,1792]{1,0:T(8,128)(2,1)} fusion(bf16[3,1792,608]{2,1,0:T(8,128)(2,1)} %all-gather.2.cloned.1.call-done, f32[768,608]{0,1:T(8,128)} %fusion.16, bf16[768,1792]{1,0:T(8,128)(2,1)} %get-tuple-element.10, f32[1792]{0:T(1024)S(1)} %convert_element_type.123, f32[768]{0:T(1024)S(1)} %add_rsqrt_fusion), kind=kOutput, calls=%fused_computation.20 | convolution fusion | flops 3356737536 | bytes 11970560 | tf_op jit(solution)/shard_map/tf,df->td/dot_general | solution.py:164
  269.4 0.0 reduce-scatter.2.cloned.1.call-update
  269.4 36.0 %reduce-scatter.2.cloned.1.call-done = bf16[96,1792]{1,0:T(8,128)(2,1)} async-done(((bf16[768,1792]{1,0:T(8,128)(2,1)}), bf16[96,1792]{1,0:T(8,128)(2,1)}) %reduce-scatter.2.cloned.1.call-update) | async-done | bytes 344080 | tf_op jit(solution)/shard_map/reduce_scatter | solution.py:168
  305.4 1.9 add_convert_fusion.1
  (40 shorter events, 0.3 us)
Async XLA Ops:
  7.4 35.5 %copy-start = (bf16[3,224,1792]{2,1,0:T(8,128)(2,1)S(1)}, bf16[3,224,1792]{2,1,0:T(8,128)(2,1)}, u32[]{:S(2)}) copy-start(bf16[3,224,1792]{2,1,0:T(8,128)(2,1)} %param.16) | copy-start | bytes 7225348
  30.5 11.9 %copy-start.9 = (s32[1,24]{1,0:T(1,128)S(1)}, s32[1,24]{1,0:T(1,128)}, u32[]{:S(2)}) copy-start(s32[1,24]{1,0:T(1,128)} %param.25) | copy-start | bytes 292
  30.5 105.7 %all-to-all-start = ((bf16[32,2,64,2,224]{4,2,3,1,0:T(8,128)(2,1)}), bf16[32,2,64,2,224]{4,2,3,1,0:T(8,128)(2,1)}, u32[]{:S(2)}, u32[]{:S(2)}) async-start(bf16[32,2,64,2,224]{4,2,3,1,0:T(8,128)(2,1)} %bitcast.75), calls=%async_computation | async-start | bytes 8388608 | tf_op jit(solution)/shard_map/all_to_all | solution.py:111
  42.4 191.2 %all-reduce.2.cloned.1.call-start = ((), (), s32[]{:S(2)}) async-start(), calls=%async_computation.2 | async-start | bytes 5505024 | tf_op jit(solution)/shard_map/psum | solution.py:153
  42.9 5.3 %copy-start.7 = (s32[768]{0:T(1024)S(1)}, s32[768]{0:T(1024)}, u32[]{:S(2)}) copy-start(s32[768]{0:T(1024)} %param.24) | copy-start | bytes 9220
  42.9 5.4 %copy-start.4 = (bf16[8,1792,16]{1,2,0:T(8,128)(2,1)S(1)}, bf16[8,1792,16]{1,2,0:T(8,128)(2,1)}, u32[]{:S(2)}) copy-start(bf16[8,1792,16]{1,2,0:T(8,128)(2,1)} %param.18) | copy-start | bytes 1376260
  46.8 1.3 copy-start.2
  48.2 31.5 %copy-start.11 = (f32[4]{0:T(128)S(1)}, f32[4]{0:T(128)}, u32[]{:S(2)}) copy-start(f32[4]{0:T(128)} %param.20) | copy-start | bytes 52
  48.2 31.5 %copy-start.12 = (s32[24]{0:T(128)S(1)}, s32[24]{0:T(128)}, u32[]{:S(2)}) copy-start(s32[24]{0:T(128)} %param.26) | copy-start | bytes 292
  51.1 30.4 %copy-start.10 = (bf16[2,224,1024]{2,1,0:T(8,128)(2,1)S(1)}, bf16[2,224,1024]{2,1,0:T(8,128)(2,1)}, u32[]{:S(2)}) copy-start(bf16[2,224,1024]{2,1,0:T(8,128)(2,1)} %param.19) | copy-start | bytes 2752516
  139.6 1.6 copy-start.6
  141.3 9.6 %copy-start.5 = (bf16[768,2,112]{0,2,1:T(8,128)(2,1)S(1)}, bf16[768,2,112]{0,2,1:T(8,128)(2,1)}, u32[]{:S(2)}) copy-start(bf16[768,2,112]{0,2,1:T(8,128)(2,1)} %get-tuple-element.17) | copy-start | bytes 1032196
  150.9 7.6 %copy-start.3 = (bf16[224,1792]{1,0:T(8,128)(2,1)S(1)}, bf16[224,1792]{1,0:T(8,128)(2,1)}, u32[]{:S(2)}) copy-start(bf16[224,1792]{1,0:T(8,128)(2,1)} %param.17) | copy-start | bytes 2408452
  158.4 3.4 %copy-start.8 = (bf16[1792]{0:T(1024)(128)(2,1)S(1)}, bf16[1792]{0:T(1024)(128)(2,1)}, u32[]{:S(2)}) copy-start(bf16[1792]{0:T(1024)(128)(2,1)} %param.21) | copy-start | bytes 10756
  161.0 92.0 %all-gather.2.cloned.1.call-start = ((), (), s32[]{:S(2)}) async-start(), calls=%async_computation.3 | async-start | bytes 7096320 | tf_op jit(solution)/shard_map/all_gather | solution.py:159
  161.6 143.8 %reduce-scatter.2.cloned.1.call-start = ((), (), s32[]{:S(2)}) async-start(), calls=%async_computation.4 | async-start | bytes 3096576 | tf_op jit(solution)/shard_map/reduce_scatter | solution.py:168
  258.9 48.4 %copy-start.1 = (bf16[3,224,1792]{2,1,0:T(8,128)(2,1)S(1)}, bf16[3,224,1792]{2,1,0:T(8,128)(2,1)}, u32[]{:S(2)}) copy-start(bf16[3,224,1792]{2,1,0:T(8,128)(2,1)} %param.16) | copy-start | bytes 7225348
Sparse Core Ops, SparseCore 0:
  161.1 72.4 all-reduce.1
  269.5 35.7 reduce-scatter.1
Sparse Core Ops, SparseCore 1:
  164.5 88.5 all-gather.1
where the time goes:
time: 315 us
  waiting for transfers between devices  172 us (55%)
  matrix products  56.8 us (18%)
  blocking collectives  26.8 us (9%)
  local copies, waits for them, and re-layouts  17.7 us (6%)
  between operations  15.2 us (5%)
  other arithmetic  14 us (4%)
  starting transfers between devices  12.2 us (4%)
    psum x1, waiting for transfers between devices, per_device(): lax.psum(attn_part.astype(jnp.bfloat16), 'mdl').astype(jnp.float32)  71.7 us
    all_to_all x1, waiting for transfers between devices, per_device(): lax.all_to_all(source_pages, 'req', split_axis=0, concat_axis=0, tiled=True)  49.7 us
    reduce_scatter x1, waiting for transfers between devices, per_device(): lax.psum_scatter(mlp_part.astype(jnp.bfloat16), 'mdl', scatter_dimension=...  36 us
    psum x1, blocking collectives, per_device(): rank_feat = lax.psum(rank_part.astype(jnp.bfloat16), 'mdl')  26.8 us
    all_gather x1, waiting for transfers between devices, per_device(): full_mlp = lax.all_gather(feedforward_weight, 'req', axis=1, tiled=True)  14.1 us
    dot_general x1, matrix products, per_device(): jnp.einsum('skcr,srj->sjkc', pages, window_pick, preferred_element_type=j...  13.2 us
    all_to_all x1, starting transfers between devices, per_device(): lax.all_to_all(source_pages, 'req', split_axis=0, concat_axis=0, tiled=True)  11.9 us
    dot_general x1, matrix products, per_device(): jnp.einsum('tf,df->td', hidden, full_mlp[2], preferred_element_type=jnp.f...  10.5 us
  transfers between devices with their start and end apart: 4, of which 4 were waited for; matrix products, arithmetic and copies ran while one was open for 7% of the time, Pallas kernels for 0%

commit v1 on v0

--- a/solution.py
+++ b/solution.py
@@ -156,7 +156,9 @@
     mean_sq = jnp.mean(resid_wide * resid_wide, axis=1, keepdims=True)
     normed = (resid_wide * lax.rsqrt(mean_sq + 1e-06) * gain_wide).astype(jnp.bfloat16)
     resid_mine = lax.dynamic_slice_in_dim(resid_full, mdl_index * row_share, row_share, 0)
-    full_mlp = lax.all_gather(feedforward_weight, "req", axis=1, tiled=True)
+    full_mlp = jnp.concatenate(
+        lax.all_to_all(jnp.stack([feedforward_weight] * lax.axis_size("req")), "req", 0, 0), axis=1
+    )
     gate_part = jnp.dot(normed, full_mlp[0], preferred_element_type=jnp.float32)
     up_part = jnp.dot(normed, full_mlp[1], preferred_element_type=jnp.float32)
     hidden = (jax.nn.silu(gate_part) * up_part).astype(jnp.bfloat16)

time: 315 us -> 362 us (1.15)
  blocking collectives: 26.8 us -> 133 us
  waiting for transfers between devices: 172 us -> 115 us
  local copies, waits for them, and re-layouts: 17.7 us -> 27 us
  starting transfers between devices: 12.2 us -> 6.05 us
  matrix products: 56.8 us -> 52.9 us
    all_to_all x0 -> x1, blocking collectives: none -> 107 us  [per_device(): lax.all_to_all(source_pages, 'req', split_axis=0, concat_axis=0, tiled=True)]
    all_to_all x1, waiting for transfers between devices: 49.7 us -> 3.64 us  [per_device(): lax.all_to_all(jnp.stack([feedforward_weight] * lax.axis_size('req')), 'r...]
    all_gather x1 -> x0, waiting for transfers between devices: 14.1 us -> none  [per_device(): full_mlp = lax.all_gather(feedforward_weight, 'req', axis=1, tiled=True)]
    all_to_all x1, starting transfers between devices: 11.9 us -> 5.74 us  [per_device(): lax.all_to_all(jnp.stack([feedforward_weight] * lax.axis_size('req')), 'r...]
    slice x0 -> x1, local copies, waits for them, and re-layouts: none -> 5.91 us  [per_device(): up_part = jnp.dot(normed, full_mlp[1], preferred_element_type=jnp.float32)]
  transfers between devices with their start and end apart: 4 -> 3, of which waited for: 4 -> 3; matrix products, arithmetic and copies ran while one was open for 7% -> 13% of each run, Pallas kernels for 0% -> 0%
where the time goes in v1:
time: 362 us
  blocking collectives  133 us (37%)
  waiting for transfers between devices  115 us (32%)
  matrix products  52.9 us (15%)
  local copies, waits for them, and re-layouts  27 us (7%)
  other arithmetic  13.8 us (4%)
  between operations  13.8 us (4%)
  starting transfers between devices  6.05 us (2%)
    all_to_all x1, blocking collectives, per_device(): lax.all_to_all(source_pages, 'req', split_axis=0, concat_axis=0, tiled=True)  107 us
    psum x1, waiting for transfers between devices, per_device(): lax.psum(attn_part.astype(jnp.bfloat16), 'mdl').astype(jnp.float32)  72.9 us
    reduce_scatter x1, waiting for transfers between devices, per_device(): lax.psum_scatter(mlp_part.astype(jnp.bfloat16), 'mdl', scatter_dimension=...  38.9 us
    psum x1, blocking collectives, per_device(): rank_feat = lax.psum(rank_part.astype(jnp.bfloat16), 'mdl')  25.6 us
    dot_general x1, matrix products, per_device(): jnp.einsum('skcr,srj->sjkc', pages, window_pick, preferred_element_type=j...  11.7 us
    dot_general x1, matrix products, per_device(): jnp.einsum('tf,df->td', hidden, full_mlp[2], preferred_element_type=jnp.f...  10.6 us
    sub x1, matrix products, per_device(): exp_scores = jnp.exp(masked - row_max)  9.56 us
    dot_general x1, matrix products, per_device(): jnp.einsum('hts,shd->thd', weights, value_heads, preferred_element_type=j...  7.56 us
  transfers between devices with their start and end apart: 3, of which 3 were waited for; matrix products, arithmetic and copies ran while one was open for 13% of the time, Pallas kernels for 0%

profile of v1, /device:TPU:8, one launch (start us, length us, event | category | flops | bytes accessed | tf_op | source)
XLA Modules:
  0.0 361.8 jit_solution(2476705083671823541)
XLA Ops:
  6.5 0.8 fusion.38
  7.4 0.1 reshape.204
  7.5 0.1 copy.24
  7.5 0.2 reduce_window_sum.18
  7.7 0.1 copy.23
  7.8 0.8 mul.159
  8.6 0.1 copy.25
  8.7 0.8 mul.162
  9.4 0.1 copy.27
  9.5 0.1 copy.28
  9.6 0.1 reshape.207
  9.8 0.1 copy.26
  9.8 0.1 sub.51
  10.0 0.1 iota_add_fusion
  10.0 6.5 %gather_fusion = bf16[64,2,224,128]{3,2,1,0:T(8,128)(2,1)} fusion(bf16[32,2,224,128]{3,2,1,0:T(8,128)(2,1)} %param.23, s32[1024]{0:T(1024)S(1)} %pad_clamp_fusion.1), kind=kCustom, calls=%fused_computation | custom fusion | bytes 14680320 | tf_op jit(solution)/shard_map/jit(_take)/gather | solution.py:100
  16.5 11.7 %convolution_convert_fusion.2 = bf16[64,64,2,224]{3,1,2,0:T(8,128)(2,1)S(1)} fusion(bf16[64,2,224,128]{3,2,1,0:T(8,128)(2,1)} %gather_fusion, s32[64,64]{1,0:T(8,128)S(1)} %iota_add_fusion), kind=kOutput, calls=%fused_computation.23 | convolution fusion | flops 472121344 | bytes 11026432 | tf_op jit(solution)/shard_map/skcr,srj->sjkc/dot_general | solution.py:107
  28.3 107.2 %all_to_all.10 = bf16[32,2,64,2,224]{4,2,3,1,0:T(8,128)(2,1)} all-to-all(bf16[32,2,64,2,224]{4,2,3,1,0:T(8,128)(2,1)S(1)} %bitcast.69), channel_id=1, replica_groups=mesh['req'=32,'mdl'=8] {'req'}, dimensions={0} | all-to-all | bytes 7340032 | tf_op jit(solution)/shard_map/all_to_all | solution.py:111
  135.5 3.4 stack.2
  138.9 5.7 %all-to-all-start.1 = ((bf16[32,3,56,608]{3,2,1,0:T(8,128)(2,1)}), bf16[32,3,56,608]{3,2,1,0:T(8,128)(2,1)}, u32[]{:S(2)}, u32[]{:S(2)}) async-start(bf16[32,3,56,608]{3,2,1,0:T(8,128)(2,1)} %stack.2), calls=%async_computation.1 | async-start | bytes 13762560 | tf_op jit(solution)/shard_map/all_to_all | solution.py:160
  144.7 0.0 all-reduce.2.cloned.1.call-start
  144.7 0.1 copy.21
  144.9 0.1 reduce
  145.0 0.1 eq.156
  145.1 0.1 ge.45
  145.1 3.9 %fusion.17 = f32[3,768,224]{1,2,0:T(8,128)S(1)} fusion(bf16[3,224,1792]{2,1,0:T(8,128)(2,1)S(1)} %copy-done, bf16[768,1792]{1,0:T(8,128)(2,1)} %param.15), kind=kOutput, calls=%fused_computation.32 | convolution fusion | flops 1849688064 | bytes 7225344 | tf_op jit(solution)/shard_map/td,kcd->ktc/dot_general | solution.py:39
  149.0 1.3 copy-done.3
  150.4 0.0 copy-start.13
  150.4 0.1 compare_convert_fusion
  150.5 2.8 fusion.55
  153.4 25.6 %psum.14 = bf16[768,16]{0,1:T(8,128)(2,1)S(1)} all-reduce(bf16[768,16]{0,1:T(8,128)(2,1)S(1)} %multiply_reduce_fusion), channel_id=1, replica_groups=mesh['req'=32,'mdl'=8] {'mdl'}, use_global_device_ids=true, to_apply=%region_4.5 | all-reduce | flops 12288 | bytes 49152 | tf_op jit(solution)/shard_map/psum | solution.py:54
  179.0 0.8 fusion.41
  179.7 0.2 convert_reduce_fusion
  179.9 0.8 fusion.40
  180.7 0.1 select_reduce_fusion.3
  180.8 0.1 select_reduce_fusion.2
  180.9 0.1 select_reduce_fusion.1
  181.0 0.1 broadcast_multiply_fusion
  181.1 1.4 fusion.51
  182.6 0.9 fusion.56
  183.5 0.1 fusion.53
  183.6 0.3 fusion.14
  183.9 1.0 add_convert_fusion.3
  184.9 1.2 compare_and_fusion
  186.2 1.4 pad_add_fusion
  187.5 2.8 gather_fusion.1
  190.4 0.2 fusion.52
  190.6 0.4 concatenate.18
  191.0 0.6 copy.30
  191.6 0.4 concatenate.15
  192.0 0.6 copy.29
  192.6 9.6 %fusion.54 = (f32[2,768]{1,0:T(2,128)S(1)}, f32[2,768,2304]{2,1,0:T(8,128)}) fusion(pred[768,2304]{1,0:T(8,128)(4,1)} %pad_add_fusion, bf16[768,2,112]{0,2,1:T(8,128)(2,1)S(1)} %copy-done.7, bf16[1536,2,112]{0,2,1:T(8,128)(2,1)S(1)} %copy.30, bf16[768,2,112]{0,2,1:T(8,128)(2,1)S(1)} %bitcast.81), kind=kOutput, calls=%fused_computation.93 | convolution fusion | flops 808945920 | bytes 17307648 | tf_op jit(solution)/shard_map/sub | solution.py:140
  202.2 7.6 %fusion.22 = bf16[2,112,768]{2,1,0:T(8,128)(2,1)S(1)} fusion(f32[2,768,2304]{2,1,0:T(8,128)} %get-tuple-element.23, f32[2,768]{1,0:T(2,128)S(1)} %get-tuple-element.22, bf16[1536,2,112]{0,2,1:T(8,128)(2,1)S(1)} %copy.29, bf16[768,2,112]{0,2,1:T(8,128)(2,1)S(1)} %copy-done.6), kind=kOutput, calls=%fused_computation.34 | convolution fusion | flops 802037760 | bytes 15538176 | tf_op jit(solution)/shard_map/hts,shd->thd/dot_general | solution.py:143
  209.8 2.5 convolution_convert_fusion
  212.3 0.0 all-reduce.2.cloned.1.call-update
  212.3 0.3 reduce-scatter.2.cloned.1.call-start
  212.6 72.9 %all-reduce.2.cloned.1.call-done = bf16[768,1792]{1,0:T(8,128)(2,1)} async-done(((bf16[768,1792]{1,0:T(8,128)(2,1)}), bf16[768,1792]{1,0:T(8,128)(2,1)}) %all-reduce.2.cloned.1.call-update) | async-done | bytes 2752528 | tf_op jit(solution)/shard_map/psum | solution.py:153
  285.5 5.1 %fusion.6 = (f32[768]{0:T(1024)S(1)}, bf16[768,1792]{1,0:T(8,128)(2,1)}) fusion(bf16[768,1792]{1,0:T(8,128)(2,1)} %all-reduce.2.cloned.1.call-done, bf16[768,1792]{1,0:T(8,128)(2,1)} %param.15), kind=kLoop, calls=%fused_computation.14 | loop fusion | flops 9633024 | bytes 8260608 | tf_op jit(solution)/shard_map/reduce_sum | solution.py:156
  290.6 3.6 %all-to-all-done.1 = bf16[32,3,56,608]{3,2,1,0:T(8,128)(2,1)} async-done(((bf16[32,3,56,608]{3,2,1,0:T(8,128)(2,1)}), bf16[32,3,56,608]{3,2,1,0:T(8,128)(2,1)}, u32[]{:S(2)}, u32[]{:S(2)}) %all-to-all-start.1) | async-done | bytes 6537248 | tf_op jit(solution)/shard_map/all_to_all | solution.py:160
  294.3 5.9 %fusion.50 = (bf16[1,32,56,608]{3,2,0,1:T(8,128)(2,1)}, bf16[1,32,56,608]{3,2,0,1:T(8,128)(2,1)}, bf16[1,32,56,608]{3,2,0,1:T(8,128)(2,1)S(1)}) fusion(bf16[3,32,56,608]{3,2,0,1:T(8,128)(2,1)} %bitcast.23), kind=kLoop, calls=%fused_computation.89 | loop fusion | bytes 13074432 | tf_op jit(solution)/shard_map/slice | solution.py:163
  300.2 3.4 fusion.28
  303.6 10.6 %convolution_convert_fusion.1 = bf16[768,1792]{1,0:T(8,128)(2,1)} fusion(bf16[1792,608]{1,0:T(8,128)(2,1)} %bitcast.76, f32[768,608]{0,1:T(8,128)} %fusion.28, bf16[1792,608]{1,0:T(8,128)(2,1)} %bitcast.75, bf16[768,1792]{1,0:T(8,128)(2,1)} %get-tuple-element.10, f32[1792]{0:T(1024)S(1)} %convert_element_type.123, f32[768]{0:T(1024)S(1)} %add_rsqrt_fusion), kind=kOutput, calls=%fused_computation.20 | convolution fusion | flops 3356737536 | bytes 11741184 | tf_op jit(solution)/shard_map/tf,df->td/dot_general | solution.py:166
  314.2 0.0 reduce-scatter.2.cloned.1.call-update
  314.2 38.9 %reduce-scatter.2.cloned.1.call-done = bf16[96,1792]{1,0:T(8,128)(2,1)} async-done(((bf16[768,1792]{1,0:T(8,128)(2,1)}), bf16[96,1792]{1,0:T(8,128)(2,1)}) %reduce-scatter.2.cloned.1.call-update) | async-done | bytes 344080 | tf_op jit(solution)/shard_map/reduce_scatter | solution.py:170
  353.1 1.9 add_convert_fusion.1
  (44 shorter events, 0.3 us)
Async XLA Ops:
  6.5 138.6 %copy-start = (bf16[3,224,1792]{2,1,0:T(8,128)(2,1)S(1)}, bf16[3,224,1792]{2,1,0:T(8,128)(2,1)}, u32[]{:S(2)}) copy-start(bf16[3,224,1792]{2,1,0:T(8,128)(2,1)} %param.16) | copy-start | bytes 7225348
  28.3 107.2 %copy-start.8 = (bf16[3,56,608]{2,1,0:T(8,128)(2,1)S(1)}, bf16[3,56,608]{2,1,0:T(8,128)(2,1)}, u32[]{:S(2)}) copy-start(bf16[3,56,608]{2,1,0:T(8,128)(2,1)} %param.22) | copy-start | bytes 612868
  138.9 5.8 %copy-start.11 = (s32[1,24]{1,0:T(1,128)S(1)}, s32[1,24]{1,0:T(1,128)}, u32[]{:S(2)}) copy-start(s32[1,24]{1,0:T(1,128)} %param.25) | copy-start | bytes 292
  138.9 155.4 %all-to-all-start.1 = ((bf16[32,3,56,608]{3,2,1,0:T(8,128)(2,1)}), bf16[32,3,56,608]{3,2,1,0:T(8,128)(2,1)}, u32[]{:S(2)}, u32[]{:S(2)}) async-start(bf16[32,3,56,608]{3,2,1,0:T(8,128)(2,1)} %stack.2), calls=%async_computation.1 | async-start | bytes 13762560 | tf_op jit(solution)/shard_map/all_to_all | solution.py:160
  144.7 140.8 %all-reduce.2.cloned.1.call-start = ((), (), s32[]{:S(2)}) async-start(), calls=%async_computation.3 | async-start | bytes 5505024 | tf_op jit(solution)/shard_map/psum | solution.py:153
  145.1 5.3 %copy-start.9 = (s32[768]{0:T(1024)S(1)}, s32[768]{0:T(1024)}, u32[]{:S(2)}) copy-start(s32[768]{0:T(1024)} %param.24) | copy-start | bytes 9220
  145.1 5.4 %copy-start.5 = (bf16[8,1792,16]{1,2,0:T(8,128)(2,1)S(1)}, bf16[8,1792,16]{1,2,0:T(8,128)(2,1)}, u32[]{:S(2)}) copy-start(bf16[8,1792,16]{1,2,0:T(8,128)(2,1)} %param.18) | copy-start | bytes 1376260
  149.0 1.3 copy-start.3
  150.4 30.3 %copy-start.13 = (f32[4]{0:T(128)S(1)}, f32[4]{0:T(128)}, u32[]{:S(2)}) copy-start(f32[4]{0:T(128)} %param.20) | copy-start | bytes 52
  150.4 30.3 %copy-start.14 = (s32[24]{0:T(128)S(1)}, s32[24]{0:T(128)}, u32[]{:S(2)}) copy-start(s32[24]{0:T(128)} %param.26) | copy-start | bytes 292
  153.3 29.2 %copy-start.12 = (bf16[2,224,1024]{2,1,0:T(8,128)(2,1)S(1)}, bf16[2,224,1024]{2,1,0:T(8,128)(2,1)}, u32[]{:S(2)}) copy-start(bf16[2,224,1024]{2,1,0:T(8,128)(2,1)} %param.19) | copy-start | bytes 2752516
  191.0 1.6 copy-start.7
  192.6 9.6 %copy-start.6 = (bf16[768,2,112]{0,2,1:T(8,128)(2,1)S(1)}, bf16[768,2,112]{0,2,1:T(8,128)(2,1)}, u32[]{:S(2)}) copy-start(bf16[768,2,112]{0,2,1:T(8,128)(2,1)} %get-tuple-element.20) | copy-start | bytes 1032196
  202.2 7.6 %copy-start.4 = (bf16[224,1792]{1,0:T(8,128)(2,1)S(1)}, bf16[224,1792]{1,0:T(8,128)(2,1)}, u32[]{:S(2)}) copy-start(bf16[224,1792]{1,0:T(8,128)(2,1)} %param.17) | copy-start | bytes 2408452
  209.8 2.8 copy-start.10
  212.3 140.8 %reduce-scatter.2.cloned.1.call-start = ((), (), s32[]{:S(2)}) async-start(), calls=%async_computation.4 | async-start | bytes 3096576 | tf_op jit(solution)/shard_map/reduce_scatter | solution.py:170
  294.3 5.9 %copy-start.2 = (bf16[768,1792]{1,0:T(8,128)(2,1)S(1)}, bf16[768,1792]{1,0:T(8,128)(2,1)}, u32[]{:S(2)}) copy-start(bf16[768,1792]{1,0:T(8,128)(2,1)} %get-tuple-element.10) | copy-start | bytes 8257540
  303.6 51.4 %copy-start.1 = (bf16[3,224,1792]{2,1,0:T(8,128)(2,1)S(1)}, bf16[3,224,1792]{2,1,0:T(8,128)(2,1)}, u32[]{:S(2)}) copy-start(bf16[3,224,1792]{2,1,0:T(8,128)(2,1)} %param.16) | copy-start | bytes 7225348
Sparse Core Ops, SparseCore 0:
  212.4 73.0 all-reduce.1
  314.3 38.7 reduce-scatter.1
